TPU v7x, 32 devices: a whole 2x2x4 slice. The times are simulated.
32 devices in a mesh: grp: 4 (over y, x), dev: 8 (over z, core).
Axes of the slice: x: 2, y: 2, z: 4, core: 2. Of those that a mesh axis runs over, the one named last changes fastest.
Arguments:
- particles: float32 [128, 5, 128], P(('grp', 'dev')), as said below
- entropy: float32 [128, 128], P(('grp', 'dev')), may hold values from 0.5 to 2
- lists: int32 [128, 64], P(('grp', 'dev')), may hold values from 0 to 127, as said below
- counts: int32 [128], P(('grp', 'dev')), may hold values from 16 to 64, as said below
Outputs:
- density: float32 [128, 128], P(('grp', 'dev'))
- accel: float32 [128, 3, 128], P(('grp', 'dev'))
Inputs may be any that keep to these rules, and one draw needn't show every extreme that they name: lists[c, 0] = c; every id lies in the group of c or in one of the two groups next to it, counting groups of 32 cells around a loop. `counts`: each count is a multiple of 16. `particles`: coordinates in 0 to 1 within the group's slab, masses positive, smoothing lengths from 0.3 to 0.6.
All inputs are finite; a program needn't handle non-finite values.
Results may differ from a plain program's by a relative error of at most 0.0003.
Values sent between devices are 32-bit elements; how exact they have to be, the bound alone decides.
No kernel may reach another device: no remote copies, remote signals or barrier semaphores. Data moves between devices by JAX's collectives and lax.ppermute only.
A program may use at most 64 MiB of HBM per device.

v0:
```python
import math
import jax
import jax.numpy as jnp
from jax import lax
from jax.sharding import PartitionSpec as P

NB = 64
NBLK = 8
norm_const = 21.0 / (16.0 * math.pi)


def padded(block, sides, width):
    for axis, dim in sides:
        count = lax.axis_size(axis)
        forward = [(i, i + 1) for i in range(count - 1)]
        forward.append((count - 1, 0))
        backward = [(target, source) for source, target in forward]
        low = lax.ppermute(
            lax.slice_in_dim(block, block.shape[dim] - width, None, axis=dim), axis, forward
        )
        high = lax.ppermute(lax.slice_in_dim(block, 0, width, axis=dim), axis, backward)
        block = jnp.concatenate([low, block, high], axis=dim)
    return block


def kernel_parts(dist_sq, smooth):
    ratio = jnp.sqrt(dist_sq) / smooth
    base_of = jnp.maximum(1.0 - 0.5 * ratio, 0.0)
    kernel = norm_const / smooth**3 * base_of**4 * (1.0 + 2.0 * ratio)
    slope = -5.0 * norm_const / smooth**5 * base_of**3
    return (kernel, slope)


def on_device(particles, entropy, lists, counts):
    own_cells = particles.shape[0]
    groups = lax.axis_size("grp")
    members = lax.axis_size("dev")
    group_cells = own_cells * members
    group_at = lax.axis_index("grp")
    group_of = lists // group_cells
    within = lists % group_cells
    side_of = (group_of - group_at + 1 + groups) % groups
    shift_all = (side_of - 1).astype(jnp.float32)
    member_of = within // own_cells
    cell_of = within % own_cells
    rimmed = padded(particles, (("grp", 0),), own_cells)
    extended = lax.all_gather(rimmed, "dev", axis=0, tiled=True)
    slots_ext = member_of * (3 * own_cells) + side_of * own_cells + cell_of
    upper = NB // NBLK
    slot_range = jnp.arange(NBLK, dtype=jnp.int32)
    own_smooth = particles[:, None, 4, :, None]
    unit_first = jnp.array([1.0, 0.0, 0.0], dtype=jnp.float32)

    def fetch_block(block_at):
        chosen = lax.dynamic_slice_in_dim(slots_ext, block_at * NBLK, NBLK, 1)
        shift_blk = lax.dynamic_slice_in_dim(shift_all, block_at * NBLK, NBLK, 1)
        others = extended[chosen]
        live = ((block_at * NBLK + slot_range)[None, :] < counts[:, None]).astype(jnp.float32)
        offset = particles[:, None, :3, :, None] - others[:, :, :3, None, :]
        offset = offset - shift_blk[:, :, None, None, None] * unit_first[None, None, :, None, None]
        dist_sq = jnp.sum(offset * offset, axis=2)
        return (chosen, others, live, offset, dist_sq)

    def density_step(block_at, total):
        chosen, others, live, offset, dist_sq = fetch_block(block_at)
        kernel, slope = kernel_parts(dist_sq, own_smooth)
        return total + jnp.sum(
            live[:, :, None, None] * others[:, :, 3, None, :] * kernel, axis=(1, 3)
        )

    density = lax.fori_loop(
        0, upper, density_step, jnp.zeros((own_cells, particles.shape[2]), jnp.float32)
    )
    pressure = entropy * density ** (5.0 / 3.0)
    weight = pressure / (density * density)
    weight_rim = padded(weight, (("grp", 0),), own_cells)
    weight_ext = lax.all_gather(weight_rim, "dev", axis=0, tiled=True)

    def force_step(block_at, total):
        chosen, others, live, offset, dist_sq = fetch_block(block_at)
        kernel_i, slope_i = kernel_parts(dist_sq, own_smooth)
        kernel_j, slope_j = kernel_parts(dist_sq, others[:, :, 4, None, :])
        factor = (
            live[:, :, None, None]
            * others[:, :, 3, None, :]
            * (weight[:, None, :, None] * slope_i + weight_ext[chosen][:, :, None, :] * slope_j)
        )
        return total - jnp.sum(factor[:, :, None] * offset, axis=(1, 4))

    accel = lax.fori_loop(
        0, upper, force_step, jnp.zeros((own_cells, 3, particles.shape[2]), jnp.float32)
    )
    return (density, accel)


def solution(mesh):
    return jax.shard_map(
        on_device,
        mesh=mesh,
        in_specs=(
            P(("grp", "dev"), None, None),
            P(("grp", "dev"), None),
            P(("grp", "dev"), None),
            P(("grp", "dev")),
        ),
        out_specs=(P(("grp", "dev"), None), P(("grp", "dev"), None, None)),
        check_vma=False,
    )
```

profile of v0, /device:TPU:0, one launch (start us, length us, event | category | flops | bytes accessed | tf_op | source)
XLA Modules:
  0.0 148.0 jit_solution(8237750292582553730)
XLA Ops:
  1.3 3.9 %collective-permute-start.1 = (f32[4,5,128]{2,1,0:T(8,128)S(1)}, f32[4,5,128]{2,1,0:T(8,128)S(1)}, u32[]{:S(2)}, u32[]{:S(2)}) collective-permute-start(f32[4,5,128]{2,1,0:T(8,128)S(1)} %copy.28), channel_id=1, source_target_pairs={{8,0},{16,8},{24,16},{0,24},{9,1},{17,9},{25,17},{1,25},{10,2},{18... | collective-permute-start | bytes 30728 | tf_op jit(solution)/shard_map/ppermute | solution.py:21
  8.0 1.9 %collective-permute-done = f32[4,5,128]{2,1,0:T(8,128)S(1)} collective-permute-done((f32[4,5,128]{2,1,0:T(8,128)S(1)}, f32[4,5,128]{2,1,0:T(8,128)S(1)}, u32[]{:S(2)}, u32[]{:S(2)}) %collective-permute-start) | collective-permute-done | bytes 10272 | tf_op jit(solution)/shard_map/ppermute | solution.py:18
  9.9 14.7 %all_gather.6 = f32[96,5,128]{2,1,0:T(8,128)S(1)} all-gather(f32[12,5,128]{2,1,0:T(8,128)S(1)} %pad_maximum_fusion), channel_id=1, replica_groups=mesh['grp'=4,'dev'=8] {'dev'}, dimensions={0}, use_global_device_ids=true | all-gather | bytes 276480 | tf_op jit(solution)/shard_map/all_gather | solution.py:47
  24.6 41.9 %while.34 = (s32[]{:T(128)}, f32[4,128]{1,0:T(4,128)S(1)}, s32[4]{0:T(128)}, s32[4,64]{1,0:T(4,128)S(1)}, f32[96,5,128]{2,1,0:T(8,128)S(1)}, /*index=5*/f32[4,1,...) while((s32[]{:T(128)}, f32[4,128]{1,0:T(4,128)S(1)}, ...), condition=%wide.region_3.4_spmd.clone.clone, body=%wide.region_0.3_spmd.sunk.clone.clone.sunk | while | flops 12065039 | bytes 4628909 | solution.py:71
  28.4 1.4 multiply_reduce_fusion.9
  33.7 1.4 multiply_reduce_fusion.9
  38.9 1.4 multiply_reduce_fusion.9
  44.1 1.4 multiply_reduce_fusion.9
  49.4 1.4 multiply_reduce_fusion.9
  54.6 1.4 multiply_reduce_fusion.9
  59.9 1.4 multiply_reduce_fusion.9
  65.1 1.4 multiply_reduce_fusion.9
  68.7 1.6 %collective-permute-done.3 = f32[4,128]{1,0:T(4,128)S(1)} collective-permute-done((f32[4,128]{1,0:T(4,128)S(1)}, f32[4,128]{1,0:T(4,128)S(1)}, u32[]{:S(2)}, u32[]{:S(2)}) %collective-permute-start.3) | collective-permute-done | bytes 2080 | tf_op jit(solution)/shard_map/ppermute | solution.py:21
  70.2 2.0 %collective-permute-done.2 = f32[4,128]{1,0:T(4,128)S(1)} collective-permute-done((f32[4,128]{1,0:T(4,128)S(1)}, f32[4,128]{1,0:T(4,128)S(1)}, u32[]{:S(2)}, u32[]{:S(2)}) %collective-permute-start.2) | collective-permute-done | bytes 2080 | tf_op jit(solution)/shard_map/ppermute | solution.py:18
  72.2 14.0 %all-gather = f32[8,12,128]{2,1,0:T(8,128)S(1)} all-gather(f32[1,12,128]{2,1,0:T(8,128)S(1)} %maximum_bitcast_fusion), channel_id=1, replica_groups=mesh['grp'=4,'dev'=8] {'dev'}, dimensions={0}, use_global_device_ids=true | all-gather | bytes 55296 | tf_op jit(solution)/shard_map/all_gather | solution.py:77
  86.2 61.1 %while.35 = (s32[]{:T(128)}, f32[4,3,128]{2,1,0:T(4,128)S(1)}, s32[4]{0:T(128)}, s32[4,64]{1,0:T(4,128)S(1)}, f32[96,5,128]{2,1,0:T(8,128)S(1)}, /*index=5*/f32[...) while((s32[]{:T(128)}, f32[4,3,128]{2,1,0:T(4,128)S(1)}, ...), condition=%wide.region_7.8_spmd.clone.clone, body=%wide.region_4.7_spmd.sunk.clone.clone.sunk | while | flops 21519628 | bytes 9044925 | solution.py:90
  90.6 1.9 %fusion.24 = f32[4,8,128,128]{3,2,1,0:T(8,128)S(1)} fusion(f32[4,8,128,128]{3,2,1,0:T(8,128)S(1)} %multiply_reduce_fusion.10, f32[4,8,128]{2,1,0:T(8,128)S(1)} %bitcast.59, f32[4,8,128]{2,1,0:T(8,128)S(1)} %get-tuple-element.869, f32[4,8,128]{2,1,0:T(8,128)S(1)} %bitcast.60, f32[4,128]{1,0:T(4,128)S(1)} %bitcast.64, ...), kind=kLoop, calls=%fused_computation.25.clone.1 | loop fusion | flops 9437184 | bytes 4265984 | tf_op jit(solution)/shard_map/while/body/eval_jaxpr/mul | solution.py:84
  98.2 1.9 %fusion.24 = f32[4,8,128,128]{3,2,1,0:T(8,128)S(1)} fusion(f32[4,8,128,128]{3,2,1,0:T(8,128)S(1)} %multiply_reduce_fusion.10, f32[4,8,128]{2,1,0:T(8,128)S(1)} %bitcast.59, f32[4,8,128]{2,1,0:T(8,128)S(1)} %get-tuple-element.869, f32[4,8,128]{2,1,0:T(8,128)S(1)} %bitcast.60, f32[4,128]{1,0:T(4,128)S(1)} %bitcast.64, ...), kind=kLoop, calls=%fused_computation.25.clone.1 | loop fusion | flops 9437184 | bytes 4265984 | tf_op jit(solution)/shard_map/while/body/eval_jaxpr/mul | solution.py:84
  105.9 1.9 %fusion.24 = f32[4,8,128,128]{3,2,1,0:T(8,128)S(1)} fusion(f32[4,8,128,128]{3,2,1,0:T(8,128)S(1)} %multiply_reduce_fusion.10, f32[4,8,128]{2,1,0:T(8,128)S(1)} %bitcast.59, f32[4,8,128]{2,1,0:T(8,128)S(1)} %get-tuple-element.869, f32[4,8,128]{2,1,0:T(8,128)S(1)} %bitcast.60, f32[4,128]{1,0:T(4,128)S(1)} %bitcast.64, ...), kind=kLoop, calls=%fused_computation.25.clone.1 | loop fusion | flops 9437184 | bytes 4265984 | tf_op jit(solution)/shard_map/while/body/eval_jaxpr/mul | solution.py:84
  113.5 1.9 %fusion.24 = f32[4,8,128,128]{3,2,1,0:T(8,128)S(1)} fusion(f32[4,8,128,128]{3,2,1,0:T(8,128)S(1)} %multiply_reduce_fusion.10, f32[4,8,128]{2,1,0:T(8,128)S(1)} %bitcast.59, f32[4,8,128]{2,1,0:T(8,128)S(1)} %get-tuple-element.869, f32[4,8,128]{2,1,0:T(8,128)S(1)} %bitcast.60, f32[4,128]{1,0:T(4,128)S(1)} %bitcast.64, ...), kind=kLoop, calls=%fused_computation.25.clone.1 | loop fusion | flops 9437184 | bytes 4265984 | tf_op jit(solution)/shard_map/while/body/eval_jaxpr/mul | solution.py:84
  121.2 1.9 %fusion.24 = f32[4,8,128,128]{3,2,1,0:T(8,128)S(1)} fusion(f32[4,8,128,128]{3,2,1,0:T(8,128)S(1)} %multiply_reduce_fusion.10, f32[4,8,128]{2,1,0:T(8,128)S(1)} %bitcast.59, f32[4,8,128]{2,1,0:T(8,128)S(1)} %get-tuple-element.869, f32[4,8,128]{2,1,0:T(8,128)S(1)} %bitcast.60, f32[4,128]{1,0:T(4,128)S(1)} %bitcast.64, ...), kind=kLoop, calls=%fused_computation.25.clone.1 | loop fusion | flops 9437184 | bytes 4265984 | tf_op jit(solution)/shard_map/while/body/eval_jaxpr/mul | solution.py:84
  128.8 1.9 %fusion.24 = f32[4,8,128,128]{3,2,1,0:T(8,128)S(1)} fusion(f32[4,8,128,128]{3,2,1,0:T(8,128)S(1)} %multiply_reduce_fusion.10, f32[4,8,128]{2,1,0:T(8,128)S(1)} %bitcast.59, f32[4,8,128]{2,1,0:T(8,128)S(1)} %get-tuple-element.869, f32[4,8,128]{2,1,0:T(8,128)S(1)} %bitcast.60, f32[4,128]{1,0:T(4,128)S(1)} %bitcast.64, ...), kind=kLoop, calls=%fused_computation.25.clone.1 | loop fusion | flops 9437184 | bytes 4265984 | tf_op jit(solution)/shard_map/while/body/eval_jaxpr/mul | solution.py:84
  136.4 1.9 %fusion.24 = f32[4,8,128,128]{3,2,1,0:T(8,128)S(1)} fusion(f32[4,8,128,128]{3,2,1,0:T(8,128)S(1)} %multiply_reduce_fusion.10, f32[4,8,128]{2,1,0:T(8,128)S(1)} %bitcast.59, f32[4,8,128]{2,1,0:T(8,128)S(1)} %get-tuple-element.869, f32[4,8,128]{2,1,0:T(8,128)S(1)} %bitcast.60, f32[4,128]{1,0:T(4,128)S(1)} %bitcast.64, ...), kind=kLoop, calls=%fused_computation.25.clone.1 | loop fusion | flops 9437184 | bytes 4265984 | tf_op jit(solution)/shard_map/while/body/eval_jaxpr/mul | solution.py:84
  144.1 1.9 %fusion.24 = f32[4,8,128,128]{3,2,1,0:T(8,128)S(1)} fusion(f32[4,8,128,128]{3,2,1,0:T(8,128)S(1)} %multiply_reduce_fusion.10, f32[4,8,128]{2,1,0:T(8,128)S(1)} %bitcast.59, f32[4,8,128]{2,1,0:T(8,128)S(1)} %get-tuple-element.869, f32[4,8,128]{2,1,0:T(8,128)S(1)} %bitcast.60, f32[4,128]{1,0:T(4,128)S(1)} %bitcast.64, ...), kind=kLoop, calls=%fused_computation.25.clone.1 | loop fusion | flops 9437184 | bytes 4265984 | tf_op jit(solution)/shard_map/while/body/eval_jaxpr/mul | solution.py:84
  (276 shorter events, 81.6 us)
Async XLA Ops:
  1.3 6.7 %collective-permute-start.1 = (f32[4,5,128]{2,1,0:T(8,128)S(1)}, f32[4,5,128]{2,1,0:T(8,128)S(1)}, u32[]{:S(2)}, u32[]{:S(2)}) collective-permute-start(f32[4,5,128]{2,1,0:T(8,128)S(1)} %copy.28), channel_id=1, source_target_pairs={{8,0},{16,8},{24,16},{0,24},{9,1},{17,9},{25,17},{1,25},{10,2},{18... | collective-permute-start | bytes 30728 | tf_op jit(solution)/shard_map/ppermute | solution.py:21
  5.3 4.6 %collective-permute-start = (f32[4,5,128]{2,1,0:T(8,128)S(1)}, f32[4,5,128]{2,1,0:T(8,128)S(1)}, u32[]{:S(2)}, u32[]{:S(2)}) collective-permute-start(f32[4,5,128]{2,1,0:T(8,128)S(1)} %copy.28), channel_id=1, source_target_pairs={{0,8},{8,16},{16,24},{24,0},{1,9},{9,17},{17,25},{25,1},{2,10},{10... | collective-permute-start | bytes 30728 | tf_op jit(solution)/shard_map/ppermute | solution.py:18
  24.6 41.9 %copy-start.1 = (f32[4,128]{1,0:T(4,128)S(1)}, f32[4,128]{1,0:T(4,128)}, u32[]{:S(2)}) copy-start(f32[4,128]{1,0:T(4,128)} %param.10) | copy-start | bytes 6148
  66.6 19.7 %copy-start = (f32[4,128]{1,0:T(4,128)}, f32[4,128]{1,0:T(4,128)S(1)}, u32[]{:S(2)}) copy-start(f32[4,128]{1,0:T(4,128)S(1)} %get-tuple-element.691) | copy-start | bytes 6148
  66.6 3.6 %collective-permute-start.3 = (f32[4,128]{1,0:T(4,128)S(1)}, f32[4,128]{1,0:T(4,128)S(1)}, u32[]{:S(2)}, u32[]{:S(2)}) collective-permute-start(f32[4,128]{1,0:T(4,128)S(1)} %multiply_divide_fusion), channel_id=1, source_target_pairs={{8,0},{16,8},{24,16},{0,24},{9,1},{17,9},{25,17},{1,25},{10,2},{18... | collective-permute-start | bytes 6152 | tf_op jit(solution)/shard_map/ppermute | solution.py:21
  67.7 4.5 %collective-permute-start.2 = (f32[4,128]{1,0:T(4,128)S(1)}, f32[4,128]{1,0:T(4,128)S(1)}, u32[]{:S(2)}, u32[]{:S(2)}) collective-permute-start(f32[4,128]{1,0:T(4,128)S(1)} %multiply_divide_fusion), channel_id=1, source_target_pairs={{0,8},{8,16},{16,24},{24,0},{1,9},{9,17},{17,25},{25,1},{2,10},{10... | collective-permute-start | bytes 6152 | tf_op jit(solution)/shard_map/ppermute | solution.py:18
where the time goes:
time: 149 us; the launch traced here: 148 us
  other arithmetic  86.7 us (58%)
  blocking collectives  28.7 us (19%)
  local copies, waits for them, and re-layouts  19.1 us (13%)
  starting transfers between devices  6 us (4%)
  waiting for transfers between devices  5.4 us (4%)
    reduce_sum x16, other arithmetic, fetch_block(): dist_sq = jnp.sum(offset * offset, axis=2)  21.1 us
    mul x8, other arithmetic, force_step(): live[:, :, None, None] * others[:, :, 3, None, :]  14.8 us
    all_gather x1, blocking collectives, on_device(): extended = lax.all_gather(rimmed, 'dev', axis=0, tiled=True)  14.7 us
    all_gather x1, blocking collectives, on_device(): weight_ext = lax.all_gather(weight_rim, 'dev', axis=0, tiled=True)  14 us
    mul x16, other arithmetic, fetch_block(): shift_blk[:, :, None, None, None] * unit_first[None, None, :, None, None]  11.7 us
    convert_element_type x16, other arithmetic, fetch_block(): ((block_at * NBLK + slot_range)[None, :] < counts[:, None]).astype(jnp.fl...  11.7 us
    reduce_sum x8, other arithmetic, density_step(): jnp.sum(live[:, :, None, None] * others[:, :, 3, None, :] * kernel, axis=...  11.5 us
    reduce_sum x8, other arithmetic, force_step(): return total - jnp.sum(factor[:, :, None] * offset, axis=(1, 4))  11.1 us
  transfers between devices with their start and end apart: 4, of which 3 were waited for; matrix products, arithmetic and copies ran while one was open for 2% of the time, Pallas kernels for 0%

commit v1 on v0

--- a/solution.py
+++ b/solution.py
@@ -44,7 +44,25 @@
     member_of = within // own_cells
     cell_of = within % own_cells
     rimmed = padded(particles, (("grp", 0),), own_cells)
-    extended = lax.all_gather(rimmed, "dev", axis=0, tiled=True)
+    t0 = rimmed
+    now = lax.axis_size("dev")
+    odd = lax.axis_index("dev")
+    field_out, z2, base_arr = (now, odd, t0.shape[0])
+    extended = lax.dynamic_update_slice_in_dim(
+        jnp.zeros(
+            [jj * field_out if dev == 0 else jj for dev, jj in enumerate(t0.shape)], t0.dtype
+        ),
+        t0,
+        z2 * base_arr,
+        axis=0,
+    )
+    for k0 in range(1, field_out):
+        t0 = lax.ppermute(
+            t0, axis_name="dev", perm=[(dev, (dev + 1) % field_out) for dev in range(field_out)]
+        )
+        extended = lax.dynamic_update_slice_in_dim(
+            extended, t0, (z2 - k0) % field_out * base_arr, axis=0
+        )
     slots_ext = member_of * (3 * own_cells) + side_of * own_cells + cell_of
     upper = NB // NBLK
     slot_range = jnp.arange(NBLK, dtype=jnp.int32)

time: 149 us -> 172 us (1.15)
  waiting for transfers between devices: 5.4 us -> 42.4 us
  blocking collectives: 28.7 us -> 14 us
    ppermute x0 -> x7, waiting for transfers between devices: none -> 37 us  [on_device(): lax.ppermute(t0, axis_name='dev', perm=[(dev, (dev + 1) % field_out) for...]
    all_gather x1 -> x0, blocking collectives: 14.7 us -> none  [on_device(): extended = lax.all_gather(rimmed, 'dev', axis=0, tiled=True)]
  transfers between devices with their start and end apart: 4 -> 11, of which waited for: 3 -> 10; matrix products, arithmetic and copies ran while one was open for 2% -> 2% of each run, Pallas kernels for 0% -> 0%
where the time goes in v1:
time: 172 us; the launch traced here: 171 us
  other arithmetic  86.7 us (50%)
  waiting for transfers between devices  42.4 us (25%)
  local copies, waits for them, and re-layouts  19.9 us (12%)
  blocking collectives  14 us (8%)
  starting transfers between devices  6.02 us (4%)
    ppermute x7, waiting for transfers between devices, on_device(): lax.ppermute(t0, axis_name='dev', perm=[(dev, (dev + 1) % field_out) for...  37 us
    reduce_sum x16, other arithmetic, fetch_block(): dist_sq = jnp.sum(offset * offset, axis=2)  21.1 us
    mul x8, other arithmetic, force_step(): live[:, :, None, None] * others[:, :, 3, None, :]  14.8 us
    all_gather x1, blocking collectives, on_device(): weight_ext = lax.all_gather(weight_rim, 'dev', axis=0, tiled=True)  14 us
    mul x16, other arithmetic, fetch_block(): shift_blk[:, :, None, None, None] * unit_first[None, None, :, None, None]  11.7 us
    convert_element_type x16, other arithmetic, fetch_block(): ((block_at * NBLK + slot_range)[None, :] < counts[:, None]).astype(jnp.fl...  11.6 us
    reduce_sum x8, other arithmetic, density_step(): jnp.sum(live[:, :, None, None] * others[:, :, 3, None, :] * kernel, axis=...  11.5 us
    reduce_sum x8, other arithmetic, force_step(): return total - jnp.sum(factor[:, :, None] * offset, axis=(1, 4))  11.1 us
  transfers between devices with their start and end apart: 11, of which 10 were waited for; matrix products, arithmetic and copies ran while one was open for 2% of the time, Pallas kernels for 0%

profile of v1, /device:TPU:0, one launch (start us, length us, event | category | flops | bytes accessed | tf_op | source)
XLA Modules:
  0.0 171.2 jit_solution(13830281718002956326)
XLA Ops:
  1.3 3.9 %collective-permute-start.1 = (f32[4,5,128]{2,1,0:T(8,128)S(1)}, f32[4,5,128]{2,1,0:T(8,128)S(1)}, u32[]{:S(2)}, u32[]{:S(2)}) collective-permute-start(f32[4,5,128]{2,1,0:T(8,128)S(1)} %copy.28), channel_id=1, source_target_pairs={{8,0},{16,8},{24,16},{0,24},{9,1},{17,9},{25,17},{1,25},{10,2},{18... | collective-permute-start | bytes 30728 | tf_op jit(solution)/shard_map/ppermute | solution.py:21
  8.0 1.9 %collective-permute-done = f32[4,5,128]{2,1,0:T(8,128)S(1)} collective-permute-done((f32[4,5,128]{2,1,0:T(8,128)S(1)}, f32[4,5,128]{2,1,0:T(8,128)S(1)}, u32[]{:S(2)}, u32[]{:S(2)}) %collective-permute-start) | collective-permute-done | bytes 10272 | tf_op jit(solution)/shard_map/ppermute | solution.py:18
  10.7 5.2 %collective-permute-done.2 = f32[12,5,128]{2,1,0:T(8,128)S(1)} collective-permute-done((f32[12,5,128]{2,1,0:T(8,128)S(1)}, f32[12,5,128]{2,1,0:T(8,128)S(1)}, u32[]{:S(2)}, u32[]{:S(2)}) %collective-permute-start.2) | collective-permute-done | bytes 30752 | tf_op jit(solution)/shard_map/ppermute | solution.py:60
  15.9 5.3 %collective-permute-done.3 = f32[12,5,128]{2,1,0:T(8,128)S(1)} collective-permute-done((f32[12,5,128]{2,1,0:T(8,128)S(1)}, f32[12,5,128]{2,1,0:T(8,128)S(1)}, u32[]{:S(2)}, u32[]{:S(2)}) %collective-permute-start.3) | collective-permute-done | bytes 30752 | tf_op jit(solution)/shard_map/ppermute | solution.py:60
  21.3 5.3 %collective-permute-done.4 = f32[12,5,128]{2,1,0:T(8,128)S(1)} collective-permute-done((f32[12,5,128]{2,1,0:T(8,128)S(1)}, f32[12,5,128]{2,1,0:T(8,128)S(1)}, u32[]{:S(2)}, u32[]{:S(2)}) %collective-permute-start.4) | collective-permute-done | bytes 30752 | tf_op jit(solution)/shard_map/ppermute | solution.py:60
  26.6 5.3 %collective-permute-done.5 = f32[12,5,128]{2,1,0:T(8,128)S(1)} collective-permute-done((f32[12,5,128]{2,1,0:T(8,128)S(1)}, f32[12,5,128]{2,1,0:T(8,128)S(1)}, u32[]{:S(2)}, u32[]{:S(2)}) %collective-permute-start.5) | collective-permute-done | bytes 30752 | tf_op jit(solution)/shard_map/ppermute | solution.py:60
  31.9 5.3 %collective-permute-done.6 = f32[12,5,128]{2,1,0:T(8,128)S(1)} collective-permute-done((f32[12,5,128]{2,1,0:T(8,128)S(1)}, f32[12,5,128]{2,1,0:T(8,128)S(1)}, u32[]{:S(2)}, u32[]{:S(2)}) %collective-permute-start.6) | collective-permute-done | bytes 30752 | tf_op jit(solution)/shard_map/ppermute | solution.py:60
  37.2 5.3 %collective-permute-done.7 = f32[12,5,128]{2,1,0:T(8,128)S(1)} collective-permute-done((f32[12,5,128]{2,1,0:T(8,128)S(1)}, f32[12,5,128]{2,1,0:T(8,128)S(1)}, u32[]{:S(2)}, u32[]{:S(2)}) %collective-permute-start.7) | collective-permute-done | bytes 30752 | tf_op jit(solution)/shard_map/ppermute | solution.py:60
  42.5 5.3 %collective-permute-done.8 = f32[12,5,128]{2,1,0:T(8,128)S(1)} collective-permute-done((f32[12,5,128]{2,1,0:T(8,128)S(1)}, f32[12,5,128]{2,1,0:T(8,128)S(1)}, u32[]{:S(2)}, u32[]{:S(2)}) %collective-permute-start.8) | collective-permute-done | bytes 30752 | tf_op jit(solution)/shard_map/ppermute | solution.py:60
  47.8 41.9 %while.34 = (s32[]{:T(128)}, f32[4,128]{1,0:T(4,128)S(1)}, s32[4]{0:T(128)}, s32[4,64]{1,0:T(4,128)S(1)}, f32[96,5,128]{2,1,0:T(8,128)S(1)}, /*index=5*/f32[4,1,...) while((s32[]{:T(128)}, f32[4,128]{1,0:T(4,128)S(1)}, ...), condition=%wide.region_3.4_spmd.clone.clone, body=%wide.region_0.3_spmd.sunk.clone.clone.sunk | while | flops 12065039 | bytes 4628909 | solution.py:89
  51.6 1.4 multiply_reduce_fusion.9
  62.1 1.4 multiply_reduce_fusion.9
  91.9 1.6 collective-permute-done.10
  93.4 2.0 %collective-permute-done.9 = f32[4,128]{1,0:T(4,128)S(1)} collective-permute-done((f32[4,128]{1,0:T(4,128)S(1)}, f32[4,128]{1,0:T(4,128)S(1)}, u32[]{:S(2)}, u32[]{:S(2)}) %collective-permute-start.9) | collective-permute-done | bytes 2080 | tf_op jit(solution)/shard_map/ppermute | solution.py:18
  95.4 14.0 %all-gather = f32[8,12,128]{2,1,0:T(8,128)S(1)} all-gather(f32[1,12,128]{2,1,0:T(8,128)S(1)} %maximum_bitcast_fusion), channel_id=1, replica_groups=mesh['grp'=4,'dev'=8] {'dev'}, dimensions={0}, use_global_device_ids=true | all-gather | bytes 55296 | tf_op jit(solution)/shard_map/all_gather | solution.py:95
  109.4 61.2 %while.35 = (s32[]{:T(128)}, f32[4,3,128]{2,1,0:T(4,128)S(1)}, s32[4]{0:T(128)}, s32[4,64]{1,0:T(4,128)S(1)}, f32[96,5,128]{2,1,0:T(8,128)S(1)}, /*index=5*/f32[...) while((s32[]{:T(128)}, f32[4,3,128]{2,1,0:T(4,128)S(1)}, ...), condition=%wide.region_7.8_spmd.clone.clone, body=%wide.region_4.7_spmd.sunk.clone.clone.sunk | while | flops 21519628 | bytes 9044925 | solution.py:108
  113.8 1.9 %fusion.24 = f32[4,8,128,128]{3,2,1,0:T(8,128)S(1)} fusion(f32[4,8,128,128]{3,2,1,0:T(8,128)S(1)} %multiply_reduce_fusion.10, f32[4,8,128]{2,1,0:T(8,128)S(1)} %bitcast.59, f32[4,8,128]{2,1,0:T(8,128)S(1)} %get-tuple-element.869, f32[4,8,128]{2,1,0:T(8,128)S(1)} %bitcast.60, f32[4,128]{1,0:T(4,128)S(1)} %bitcast.64, ...), kind=kLoop, calls=%fused_computation.25.clone.1 | loop fusion | flops 9437184 | bytes 4265984 | tf_op jit(solution)/shard_map/while/body/eval_jaxpr/mul | solution.py:102
  121.4 1.9 %fusion.24 = f32[4,8,128,128]{3,2,1,0:T(8,128)S(1)} fusion(f32[4,8,128,128]{3,2,1,0:T(8,128)S(1)} %multiply_reduce_fusion.10, f32[4,8,128]{2,1,0:T(8,128)S(1)} %bitcast.59, f32[4,8,128]{2,1,0:T(8,128)S(1)} %get-tuple-element.869, f32[4,8,128]{2,1,0:T(8,128)S(1)} %bitcast.60, f32[4,128]{1,0:T(4,128)S(1)} %bitcast.64, ...), kind=kLoop, calls=%fused_computation.25.clone.1 | loop fusion | flops 9437184 | bytes 4265984 | tf_op jit(solution)/shard_map/while/body/eval_jaxpr/mul | solution.py:102
  129.1 1.9 %fusion.24 = f32[4,8,128,128]{3,2,1,0:T(8,128)S(1)} fusion(f32[4,8,128,128]{3,2,1,0:T(8,128)S(1)} %multiply_reduce_fusion.10, f32[4,8,128]{2,1,0:T(8,128)S(1)} %bitcast.59, f32[4,8,128]{2,1,0:T(8,128)S(1)} %get-tuple-element.869, f32[4,8,128]{2,1,0:T(8,128)S(1)} %bitcast.60, f32[4,128]{1,0:T(4,128)S(1)} %bitcast.64, ...), kind=kLoop, calls=%fused_computation.25.clone.1 | loop fusion | flops 9437184 | bytes 4265984 | tf_op jit(solution)/shard_map/while/body/eval_jaxpr/mul | solution.py:102
  136.7 1.9 %fusion.24 = f32[4,8,128,128]{3,2,1,0:T(8,128)S(1)} fusion(f32[4,8,128,128]{3,2,1,0:T(8,128)S(1)} %multiply_reduce_fusion.10, f32[4,8,128]{2,1,0:T(8,128)S(1)} %bitcast.59, f32[4,8,128]{2,1,0:T(8,128)S(1)} %get-tuple-element.869, f32[4,8,128]{2,1,0:T(8,128)S(1)} %bitcast.60, f32[4,128]{1,0:T(4,128)S(1)} %bitcast.64, ...), kind=kLoop, calls=%fused_computation.25.clone.1 | loop fusion | flops 9437184 | bytes 4265984 | tf_op jit(solution)/shard_map/while/body/eval_jaxpr/mul | solution.py:102
  144.3 1.9 %fusion.24 = f32[4,8,128,128]{3,2,1,0:T(8,128)S(1)} fusion(f32[4,8,128,128]{3,2,1,0:T(8,128)S(1)} %multiply_reduce_fusion.10, f32[4,8,128]{2,1,0:T(8,128)S(1)} %bitcast.59, f32[4,8,128]{2,1,0:T(8,128)S(1)} %get-tuple-element.869, f32[4,8,128]{2,1,0:T(8,128)S(1)} %bitcast.60, f32[4,128]{1,0:T(4,128)S(1)} %bitcast.64, ...), kind=kLoop, calls=%fused_computation.25.clone.1 | loop fusion | flops 9437184 | bytes 4265984 | tf_op jit(solution)/shard_map/while/body/eval_jaxpr/mul | solution.py:102
  152.0 1.9 %fusion.24 = f32[4,8,128,128]{3,2,1,0:T(8,128)S(1)} fusion(f32[4,8,128,128]{3,2,1,0:T(8,128)S(1)} %multiply_reduce_fusion.10, f32[4,8,128]{2,1,0:T(8,128)S(1)} %bitcast.59, f32[4,8,128]{2,1,0:T(8,128)S(1)} %get-tuple-element.869, f32[4,8,128]{2,1,0:T(8,128)S(1)} %bitcast.60, f32[4,128]{1,0:T(4,128)S(1)} %bitcast.64, ...), kind=kLoop, calls=%fused_computation.25.clone.1 | loop fusion | flops 9437184 | bytes 4265984 | tf_op jit(solution)/shard_map/while/body/eval_jaxpr/mul | solution.py:102
  159.6 1.9 %fusion.24 = f32[4,8,128,128]{3,2,1,0:T(8,128)S(1)} fusion(f32[4,8,128,128]{3,2,1,0:T(8,128)S(1)} %multiply_reduce_fusion.10, f32[4,8,128]{2,1,0:T(8,128)S(1)} %bitcast.59, f32[4,8,128]{2,1,0:T(8,128)S(1)} %get-tuple-element.869, f32[4,8,128]{2,1,0:T(8,128)S(1)} %bitcast.60, f32[4,128]{1,0:T(4,128)S(1)} %bitcast.64, ...), kind=kLoop, calls=%fused_computation.25.clone.1 | loop fusion | flops 9437184 | bytes 4265984 | tf_op jit(solution)/shard_map/while/body/eval_jaxpr/mul | solution.py:102
  167.3 1.9 %fusion.24 = f32[4,8,128,128]{3,2,1,0:T(8,128)S(1)} fusion(f32[4,8,128,128]{3,2,1,0:T(8,128)S(1)} %multiply_reduce_fusion.10, f32[4,8,128]{2,1,0:T(8,128)S(1)} %bitcast.59, f32[4,8,128]{2,1,0:T(8,128)S(1)} %get-tuple-element.869, f32[4,8,128]{2,1,0:T(8,128)S(1)} %bitcast.60, f32[4,128]{1,0:T(4,128)S(1)} %bitcast.64, ...), kind=kLoop, calls=%fused_computation.25.clone.1 | loop fusion | flops 9437184 | bytes 4265984 | tf_op jit(solution)/shard_map/while/body/eval_jaxpr/mul | solution.py:102
  (300 shorter events, 91.0 us)
Async XLA Ops:
  1.3 9.3 %collective-permute-start.1 = (f32[4,5,128]{2,1,0:T(8,128)S(1)}, f32[4,5,128]{2,1,0:T(8,128)S(1)}, u32[]{:S(2)}, u32[]{:S(2)}) collective-permute-start(f32[4,5,128]{2,1,0:T(8,128)S(1)} %copy.28), channel_id=1, source_target_pairs={{8,0},{16,8},{24,16},{0,24},{9,1},{17,9},{25,17},{1,25},{10,2},{18... | collective-permute-start | bytes 30728 | tf_op jit(solution)/shard_map/ppermute | solution.py:21
  5.3 4.6 %collective-permute-start = (f32[4,5,128]{2,1,0:T(8,128)S(1)}, f32[4,5,128]{2,1,0:T(8,128)S(1)}, u32[]{:S(2)}, u32[]{:S(2)}) collective-permute-start(f32[4,5,128]{2,1,0:T(8,128)S(1)} %copy.28), channel_id=1, source_target_pairs={{0,8},{8,16},{16,24},{24,0},{1,9},{9,17},{17,25},{25,1},{2,10},{10... | collective-permute-start | bytes 30728 | tf_op jit(solution)/shard_map/ppermute | solution.py:18
  10.6 5.3 %collective-permute-start.2 = (f32[12,5,128]{2,1,0:T(8,128)S(1)}, f32[12,5,128]{2,1,0:T(8,128)S(1)}, u32[]{:S(2)}, u32[]{:S(2)}) collective-permute-start(f32[12,5,128]{2,1,0:T(8,128)S(1)} %constant_dynamic-update-slice_fusion), channel_id=1, source_target_pairs={{0,1},{1,2},{2,3},{3,4},{4,5},{5,6},{6,7},{7,0},{8,9},{9,10},{10,1... | collective-permute-start | bytes 92168 | tf_op jit(solution)/shard_map/ppermute | solution.py:60
  15.9 5.3 %collective-permute-start.3 = (f32[12,5,128]{2,1,0:T(8,128)S(1)}, f32[12,5,128]{2,1,0:T(8,128)S(1)}, u32[]{:S(2)}, u32[]{:S(2)}) collective-permute-start(f32[12,5,128]{2,1,0:T(8,128)S(1)} %collective-permute-done.2), channel_id=1, source_target_pairs={{0,1},{1,2},{2,3},{3,4},{4,5},{5,6},{6,7},{7,0},{8,9},{9,10},{10,1... | collective-permute-start | bytes 92168 | tf_op jit(solution)/shard_map/ppermute | solution.py:60
  21.2 5.3 %collective-permute-start.4 = (f32[12,5,128]{2,1,0:T(8,128)S(1)}, f32[12,5,128]{2,1,0:T(8,128)S(1)}, u32[]{:S(2)}, u32[]{:S(2)}) collective-permute-start(f32[12,5,128]{2,1,0:T(8,128)S(1)} %collective-permute-done.3), channel_id=1, source_target_pairs={{0,1},{1,2},{2,3},{3,4},{4,5},{5,6},{6,7},{7,0},{8,9},{9,10},{10,1... | collective-permute-start | bytes 92168 | tf_op jit(solution)/shard_map/ppermute | solution.py:60
  26.6 5.3 %collective-permute-start.5 = (f32[12,5,128]{2,1,0:T(8,128)S(1)}, f32[12,5,128]{2,1,0:T(8,128)S(1)}, u32[]{:S(2)}, u32[]{:S(2)}) collective-permute-start(f32[12,5,128]{2,1,0:T(8,128)S(1)} %collective-permute-done.4), channel_id=1, source_target_pairs={{0,1},{1,2},{2,3},{3,4},{4,5},{5,6},{6,7},{7,0},{8,9},{9,10},{10,1... | collective-permute-start | bytes 92168 | tf_op jit(solution)/shard_map/ppermute | solution.py:60
  31.9 5.3 %collective-permute-start.6 = (f32[12,5,128]{2,1,0:T(8,128)S(1)}, f32[12,5,128]{2,1,0:T(8,128)S(1)}, u32[]{:S(2)}, u32[]{:S(2)}) collective-permute-start(f32[12,5,128]{2,1,0:T(8,128)S(1)} %collective-permute-done.5), channel_id=1, source_target_pairs={{0,1},{1,2},{2,3},{3,4},{4,5},{5,6},{6,7},{7,0},{8,9},{9,10},{10,1... | collective-permute-start | bytes 92168 | tf_op jit(solution)/shard_map/ppermute | solution.py:60
  37.2 5.3 %collective-permute-start.7 = (f32[12,5,128]{2,1,0:T(8,128)S(1)}, f32[12,5,128]{2,1,0:T(8,128)S(1)}, u32[]{:S(2)}, u32[]{:S(2)}) collective-permute-start(f32[12,5,128]{2,1,0:T(8,128)S(1)} %collective-permute-done.6), channel_id=1, source_target_pairs={{0,1},{1,2},{2,3},{3,4},{4,5},{5,6},{6,7},{7,0},{8,9},{9,10},{10,1... | collective-permute-start | bytes 92168 | tf_op jit(solution)/shard_map/ppermute | solution.py:60
  42.5 5.3 %collective-permute-start.8 = (f32[12,5,128]{2,1,0:T(8,128)S(1)}, f32[12,5,128]{2,1,0:T(8,128)S(1)}, u32[]{:S(2)}, u32[]{:S(2)}) collective-permute-start(f32[12,5,128]{2,1,0:T(8,128)S(1)} %collective-permute-done.7), channel_id=1, source_target_pairs={{0,1},{1,2},{2,3},{3,4},{4,5},{5,6},{6,7},{7,0},{8,9},{9,10},{10,1... | collective-permute-start | bytes 92168 | tf_op jit(solution)/shard_map/ppermute | solution.py:60
  47.8 41.9 %copy-start.1 = (f32[4,128]{1,0:T(4,128)S(1)}, f32[4,128]{1,0:T(4,128)}, u32[]{:S(2)}) copy-start(f32[4,128]{1,0:T(4,128)} %param.10) | copy-start | bytes 6148
  89.7 19.6 %copy-start = (f32[4,128]{1,0:T(4,128)}, f32[4,128]{1,0:T(4,128)S(1)}, u32[]{:S(2)}) copy-start(f32[4,128]{1,0:T(4,128)S(1)} %get-tuple-element.691) | copy-start | bytes 6148
  89.8 3.6 %collective-permute-start.10 = (f32[4,128]{1,0:T(4,128)S(1)}, f32[4,128]{1,0:T(4,128)S(1)}, u32[]{:S(2)}, u32[]{:S(2)}) collective-permute-start(f32[4,128]{1,0:T(4,128)S(1)} %multiply_divide_fusion), channel_id=1, source_target_pairs={{8,0},{16,8},{24,16},{0,24},{9,1},{17,9},{25,17},{1,25},{10,2},{18... | collective-permute-start | bytes 6152 | tf_op jit(solution)/shard_map/ppermute | solution.py:21
  90.9 4.5 %collective-permute-start.9 = (f32[4,128]{1,0:T(4,128)S(1)}, f32[4,128]{1,0:T(4,128)S(1)}, u32[]{:S(2)}, u32[]{:S(2)}) collective-permute-start(f32[4,128]{1,0:T(4,128)S(1)} %multiply_divide_fusion), channel_id=1, source_target_pairs={{0,8},{8,16},{16,24},{24,0},{1,9},{9,17},{17,25},{25,1},{2,10},{10... | collective-permute-start | bytes 6152 | tf_op jit(solution)/shard_map/ppermute | solution.py:18
